TPU v7x, 32 devices: a whole 2x2x4 slice. The times are simulated.
32 devices in a mesh: wide: 8 (over y, x, core), narrow: 4 (over z).
Axes of the slice: x: 2, y: 2, z: 4, core: 2. Of those that a mesh axis runs over, the one named last changes fastest.
Arguments:
- hamiltonian_tiles: float32 [12288, 6144], P('wide', 'narrow'), may hold values from -0.0546875 to 0.0546875
- row_columns: int32 [8, 4], P('wide'), may hold values from 0 to 7, as said below
- start_vectors: float32 [12288, 128], P(('wide', 'narrow')), may hold values from -60 to 60
Outputs:
- new_vectors: float32 [12288, 128], P(('wide', 'narrow'))
Inputs may be any that keep to these rules, and one draw needn't show every extreme that they name: For block row r = w + j // 4, row_columns[w, j] = (r + d) mod 8, with d = 0 where j % 4 = 0 and, for the other tiles of that block row, distinct d between 1 and 7; a block's mirror may also be stored.
All inputs are finite; a program needn't handle non-finite values.
Results may differ from a plain program's by a relative error of at most 0.0003.
Values sent between devices are 32-bit elements; how exact they have to be, the bound alone decides.
A program may use at most 64 MiB of HBM per device.

v0:
```python
import jax
import jax.numpy as jnp
from jax import lax
from jax.sharding import PartitionSpec as P

ITERS = 2
NS_STEPS = 5


def orthonormalize(product, gram, total_rows):
    width = gram.shape[0]
    identity = jnp.eye(width, dtype=jnp.float32)
    scale = jnp.sqrt(jnp.sum(gram * gram) + 1e-06)
    current = gram / scale
    inverse = identity
    for repeat in range(NS_STEPS):
        middle = 1.5 * identity - 0.5 * jnp.dot(inverse, current, precision=lax.Precision.HIGHEST)
        current = jnp.dot(current, middle, precision=lax.Precision.HIGHEST)
        inverse = jnp.dot(middle, inverse, precision=lax.Precision.HIGHEST)
    return jnp.dot(product, inverse, precision=lax.Precision.HIGHEST) * jnp.sqrt(total_rows / scale)


def on_device(hamiltonian_tiles, row_columns, start_vectors):
    narrow_count = lax.axis_size("narrow")
    wide_count = lax.axis_size("wide")
    my_index = lax.axis_index("narrow")
    order_tile = hamiltonian_tiles.shape[0]
    slice_rows = start_vectors.shape[0]
    width = start_vectors.shape[1]
    per_row = order_tile // slice_rows
    rows_group = narrow_count // per_row
    my_block = my_index // per_row
    columns_row = row_columns[0]
    column_group = columns_row // rows_group
    column_place = columns_row % rows_group
    my_column_place = column_place[my_index]
    sender_block = jnp.arange(narrow_count, dtype=jnp.int32) // per_row
    back_weight = (
        (column_group[:, None] == jnp.arange(wide_count, dtype=jnp.int32)[None, :])
        & (column_place[:, None] == my_block)
    ).astype(jnp.float32)
    own_weight = (sender_block == my_block).astype(jnp.float32)
    total_rows = float(wide_count * rows_group * order_tile)
    vectors = start_vectors
    for repeat in range(ITERS):
        slices = lax.all_gather(vectors, "wide", axis=0, tiled=True)
        picked = jnp.take(slices.reshape(wide_count, slice_rows, width), column_group, axis=0)
        gathered_rows = lax.all_gather(vectors, "narrow", axis=0, tiled=True)
        got_column = lax.all_to_all(picked, "narrow", split_axis=0, concat_axis=0, tiled=True)
        row_block = lax.dynamic_index_in_dim(
            gathered_rows.reshape(rows_group, order_tile, width), my_block, 0, keepdims=False
        )
        column_block = lax.dynamic_index_in_dim(
            got_column.reshape(rows_group, order_tile, width), my_column_place, 0, keepdims=False
        )
        direct = jnp.dot(hamiltonian_tiles, column_block, precision=lax.Precision.HIGHEST)
        transposed = lax.dot_general(
            hamiltonian_tiles, row_block, (((0,), (0,)), ((), ())), precision=lax.Precision.HIGHEST
        )
        transposed_spread = transposed.reshape(1, per_row, slice_rows, width).reshape(
            narrow_count, slice_rows, width
        )
        direct_spread = direct.reshape(1, per_row, slice_rows, width).reshape(
            narrow_count, slice_rows, width
        )
        arrived, direct_pieces = (
            lax.all_to_all(transposed_spread, "narrow", split_axis=0, concat_axis=0, tiled=True),
            lax.all_to_all(direct_spread, "narrow", split_axis=0, concat_axis=0, tiled=True),
        )
        direct_part = jnp.einsum(
            "n,nsk->sk", own_weight, direct_pieces, precision=lax.Precision.HIGHEST
        )
        placed = jnp.einsum("nb,nsk->bsk", back_weight, arrived, precision=lax.Precision.HIGHEST)
        moved_part = lax.psum_scatter(
            placed.reshape(wide_count * slice_rows, width), "wide", scatter_dimension=0, tiled=True
        )
        product = direct_part + moved_part
        local_gram = lax.dot_general(
            product, product, (((0,), (0,)), ((), ())), precision=lax.Precision.HIGHEST
        )
        gram = lax.psum(local_gram, ("wide", "narrow"))
        vectors = orthonormalize(product, gram, total_rows)
    return vectors


def solution(mesh):
    return jax.shard_map(
        on_device,
        mesh=mesh,
        in_specs=(P("wide", "narrow"), P("wide", None), P(("wide", "narrow"), None)),
        out_specs=P(("wide", "narrow"), None),
        check_vma=False,
    )
```

profile of v0, /device:TPU:1, one launch (start us, length us, event | category | flops | bytes accessed | tf_op | source)
XLA Modules:
  0.0 499.5 jit_solution(15545345940733565304)
XLA Ops:
  7.3 18.2 %all_gather.13 = f32[1536,128]{1,0:T(8,128)S(1)} all-gather(f32[384,128]{1,0:T(8,128)} %param.7), channel_id=1, replica_groups=mesh['wide'=8,'narrow'=4] {'narrow'}, dimensions={0}, use_global_device_ids=true | all-gather | bytes 983040 | tf_op jit(solution)/shard_map/all_gather | solution.py:48
  25.5 18.1 %fusion.41 = f32[1536,128]{1,0:T(8,128)} fusion(f32[1536,1536]{1,0:T(8,128)} %param.5, f32[1536,128]{1,0:T(8,128)S(1)} %all_gather.13), kind=kOutput, calls=%fused_computation.71 | convolution fusion | flops 3623878656 | bytes 11010048 | tf_op jit(solution)/shard_map/dot_general | solution.py:57
  43.6 4.0 all-to-all-start.2
  47.7 2.0 gather_fusion
  50.7 16.3 %all-to-all-done.2 = f32[4,384,128]{2,1,0:T(8,128)S(1)} async-done(((f32[4,384,128]{2,1,0:T(8,128)}), f32[4,384,128]{2,1,0:T(8,128)S(1)}, u32[]{:S(2)}, u32[]{:S(2)}) %all-to-all-start.2) | async-done | bytes 786464 | tf_op jit(solution)/shard_map/all_to_all | solution.py:67
  66.9 3.5 all-to-all-start
  70.5 1.5 fusion.12
  73.6 16.4 %all-to-all-done = f32[4,384,128]{2,1,0:T(8,128)S(1)} async-done(((f32[4,384,128]{2,1,0:T(8,128)}), f32[4,384,128]{2,1,0:T(8,128)S(1)}, u32[]{:S(2)}, u32[]{:S(2)}) %all-to-all-start) | async-done | bytes 786464 | tf_op jit(solution)/shard_map/all_to_all | solution.py:49
  90.0 10.4 %fusion.40 = f32[128,1536]{1,0:T(8,128)S(1)} fusion(f32[1536,128]{1,0:T(8,128)S(1)} %bitcast.108, f32[1536,1536]{1,0:T(8,128)} %param.5), kind=kOutput, calls=%fused_computation.70 | convolution fusion | flops 3623878656 | bytes 11010048 | tf_op jit(solution)/shard_map/dot_general | solution.py:56
  100.5 21.5 %all_to_all.30 = f32[4,384,128]{1,2,0:T(8,128)S(1)} all-to-all(f32[4,384,128]{1,2,0:T(8,128)S(1)} %bitcast.106), channel_id=1, replica_groups=mesh['wide'=8,'narrow'=4] {'narrow'}, dimensions={0} | all-to-all | bytes 1572864 | tf_op jit(solution)/shard_map/all_to_all | solution.py:68
  125.4 121.8 %all-reduce.3.cloned.1.call-done = f32[128,128]{1,0:T(8,128)} async-done(((f32[128,128]{1,0:T(8,128)}), f32[128,128]{1,0:T(8,128)}) %all-reduce.3.cloned.1.call-update) | async-done | bytes 65552 | tf_op jit(solution)/shard_map/psum | solution.py:81
  247.2 1.5 multiply_reduce_fusion.1
  255.0 17.0 %all_gather.15 = f32[1536,128]{1,0:T(8,128)S(1)} all-gather(f32[384,128]{1,0:T(8,128)} %convolution_multiply_fusion.1), channel_id=1, replica_groups=mesh['wide'=8,'narrow'=4] {'narrow'}, dimensions={0}, use_global_device_ids=true | all-gather | bytes 983040 | tf_op jit(solution)/shard_map/all_gather | solution.py:48
  272.0 8.6 %convolution_bitcast_fusion = f32[1536,128]{0,1:T(8,128)S(1)} fusion(f32[1536,128]{1,0:T(8,128)S(1)} %all_gather.15, f32[1536,1536]{1,0:T(8,128)} %param.5), kind=kOutput, calls=%fused_computation.2 | convolution fusion | flops 3623878656 | bytes 11010048 | tf_op jit(solution)/shard_map/dot_general | solution.py:57
  281.7 4.1 all-to-all-start.5
  285.8 2.0 gather_fusion.1
  288.8 16.7 %all-to-all-done.5 = f32[4,384,128]{2,1,0:T(8,128)S(1)} async-done(((f32[4,384,128]{2,1,0:T(8,128)}), f32[4,384,128]{2,1,0:T(8,128)S(1)}, u32[]{:S(2)}, u32[]{:S(2)}) %all-to-all-start.5) | async-done | bytes 786464 | tf_op jit(solution)/shard_map/all_to_all | solution.py:67
  305.5 3.5 all-to-all-start.3
  309.3 1.5 fusion.10
  312.2 16.4 %all-to-all-done.3 = f32[4,384,128]{2,1,0:T(8,128)S(1)} async-done(((f32[4,384,128]{2,1,0:T(8,128)}), f32[4,384,128]{2,1,0:T(8,128)S(1)}, u32[]{:S(2)}, u32[]{:S(2)}) %all-to-all-start.3) | async-done | bytes 786464 | tf_op jit(solution)/shard_map/all_to_all | solution.py:49
  328.6 10.4 %fusion.50 = f32[128,1536]{1,0:T(8,128)S(1)} fusion(f32[1536,128]{1,0:T(8,128)S(1)} %bitcast.109, f32[1536,1536]{1,0:T(8,128)} %param.5), kind=kOutput, calls=%fused_computation.80 | convolution fusion | flops 3623878656 | bytes 11010048 | tf_op jit(solution)/shard_map/dot_general | solution.py:56
  339.1 21.5 %all_to_all.31 = f32[4,384,128]{1,2,0:T(8,128)S(1)} all-to-all(f32[4,384,128]{1,2,0:T(8,128)S(1)} %bitcast.107), channel_id=1, replica_groups=mesh['wide'=8,'narrow'=4] {'narrow'}, dimensions={0} | all-to-all | bytes 1572864 | tf_op jit(solution)/shard_map/all_to_all | solution.py:68
  363.9 120.9 %all-reduce.5.cloned.1.call-done = f32[128,128]{1,0:T(8,128)} async-done(((f32[128,128]{1,0:T(8,128)}), f32[128,128]{1,0:T(8,128)}) %all-reduce.5.cloned.1.call-update) | async-done | bytes 65552 | tf_op jit(solution)/shard_map/psum | solution.py:81
  484.8 1.5 multiply_reduce_fusion
  (66 shorter events, 25.0 us)
Async XLA Ops:
  6.5 41.1 %all-gather.3.cloned.1.call-start = ((), (), s32[]{:S(2)}) async-start(), calls=%async_computation.8 | async-start | bytes 1769472 | tf_op jit(solution)/shard_map/all_gather | solution.py:46
  25.5 22.1 %copy-start = (s32[1,4]{1,0:T(1,128)S(1)}, s32[1,4]{1,0:T(1,128)}, u32[]{:S(2)}) copy-start(s32[1,4]{1,0:T(1,128)} %param.6) | copy-start | bytes 52
  43.6 23.4 %all-to-all-start.2 = ((f32[4,384,128]{2,1,0:T(8,128)}), f32[4,384,128]{2,1,0:T(8,128)S(1)}, u32[]{:S(2)}, u32[]{:S(2)}) async-start(f32[4,384,128]{2,1,0:T(8,128)} %bitcast.9), calls=%async_computation.2 | async-start | bytes 1572864 | tf_op jit(solution)/shard_map/all_to_all | solution.py:67
  66.9 23.1 %all-to-all-start = ((f32[4,384,128]{2,1,0:T(8,128)}), f32[4,384,128]{2,1,0:T(8,128)S(1)}, u32[]{:S(2)}, u32[]{:S(2)}) async-start(f32[4,384,128]{2,1,0:T(8,128)} %broadcast_select_fusion.1), calls=%async_computation | async-start | bytes 1572864 | tf_op jit(solution)/shard_map/all_to_all | solution.py:49
  70.4 52.8 %reduce-scatter.3.cloned.1.call-start = ((), (), s32[]{:S(2)}) async-start(), calls=%async_computation.9 | async-start | bytes 1769472 | tf_op jit(solution)/shard_map/reduce_scatter | solution.py:74
  73.4 173.8 %all-reduce.3.cloned.1.call-start = ((), (), s32[]{:S(2)}) async-start(), calls=%async_computation.10 | async-start | bytes 131072 | tf_op jit(solution)/shard_map/psum | solution.py:81
  125.3 160.5 %all-gather.5.cloned.1.call-start = ((), (), s32[]{:S(2)}) async-start(), calls=%async_computation.11 | async-start | bytes 1769472 | tf_op jit(solution)/shard_map/all_gather | solution.py:46
  281.7 23.8 %all-to-all-start.5 = ((f32[4,384,128]{2,1,0:T(8,128)}), f32[4,384,128]{2,1,0:T(8,128)S(1)}, u32[]{:S(2)}, u32[]{:S(2)}) async-start(f32[4,384,128]{2,1,0:T(8,128)} %bitcast.17), calls=%async_computation.6 | async-start | bytes 1572864 | tf_op jit(solution)/shard_map/all_to_all | solution.py:67
  305.5 23.1 %all-to-all-start.3 = ((f32[4,384,128]{2,1,0:T(8,128)}), f32[4,384,128]{2,1,0:T(8,128)S(1)}, u32[]{:S(2)}, u32[]{:S(2)}) async-start(f32[4,384,128]{2,1,0:T(8,128)} %broadcast_select_fusion), calls=%async_computation.4 | async-start | bytes 1572864 | tf_op jit(solution)/shard_map/all_to_all | solution.py:49
  309.0 52.8 %reduce-scatter.5.cloned.1.call-start = ((), (), s32[]{:S(2)}) async-start(), calls=%async_computation.12 | async-start | bytes 1769472 | tf_op jit(solution)/shard_map/reduce_scatter | solution.py:74
  312.2 172.6 %all-reduce.5.cloned.1.call-start = ((), (), s32[]{:S(2)}) async-start(), calls=%async_computation.13 | async-start | bytes 131072 | tf_op jit(solution)/shard_map/psum | solution.py:81
Sparse Core Ops, SparseCore 0:
  9.2 28.0 all-gather.2
  74.5 40.6 reduce-scatter.2
  125.5 121.6 all-reduce.2
  255.1 25.3 all-gather.4
  312.8 39.4 reduce-scatter.4
  364.0 120.7 all-reduce.4
where the time goes:
time: 500 us
  waiting for transfers between devices  309 us (62%)
  blocking collectives  78.3 us (16%)
  matrix products  65.2 us (13%)
  starting transfers between devices  15.8 us (3%)
  between operations  15.4 us (3%)
  local copies, waits for them, and re-layouts  8.74 us (2%)
  other arithmetic  6.83 us (1%)
    psum x2, waiting for transfers between devices, on_device(): gram = lax.psum(local_gram, ('wide', 'narrow'))  243 us
    all_to_all x2, blocking collectives, on_device(): lax.all_to_all(direct_spread, 'narrow', split_axis=0, concat_axis=0, tile...  43.1 us
    all_gather x2, blocking collectives, on_device(): gathered_rows = lax.all_gather(vectors, 'narrow', axis=0, tiled=True)  35.2 us
    all_to_all x2, waiting for transfers between devices, on_device(): lax.all_to_all(transposed_spread, 'narrow', split_axis=0, concat_axis=0,...  32.9 us
    all_to_all x2, waiting for transfers between devices, on_device(): lax.all_to_all(picked, 'narrow', split_axis=0, concat_axis=0, tiled=True)  32.8 us
    dot_general x2, matrix products, on_device(): lax.dot_general(hamiltonian_tiles, row_block, (((0,), (0,)), ((), ())), p...  26.6 us
    dot_general x2, matrix products, on_device(): jnp.dot(hamiltonian_tiles, column_block, precision=lax.Precision.HIGHEST)  20.9 us
  transfers between devices with their start and end apart: 10, of which 6 were waited for; matrix products, arithmetic and copies ran while one was open for 13% of the time, Pallas kernels for 0%

commit v1 on v0

v1 whole, which is shorter than its diff:
```python
import functools

import jax
import jax.numpy as jnp
from jax import lax
from jax.experimental import pallas as pl
from jax.experimental.pallas import tpu as pltpu
from jax.sharding import PartitionSpec as P

ITERS = 2
NS_STEPS = 5
HIGHEST = lax.Precision.HIGHEST


def flip(x, mask):
    bit = 1
    while bit <= mask:
        if mask & bit:
            x = x + bit * (1 - 2 * ((x // bit) % 2))
        bit *= 2
    return x


def bits_of(count):
    bits = count.bit_length() - 1
    assert count == 1 << bits
    return bits


def orders(wide):
    bits = list(range(1, bits_of(wide)))
    return bits + [0], bits[::-1] + [0]


def position(relative, order):
    return sum(((relative >> bit) & 1) << place for place, bit in enumerate(order))


def inverse_root(gram, total):
    size = gram.shape[0]
    row = lax.broadcasted_iota(jnp.int32, (size, size), 0)
    column = lax.broadcasted_iota(jnp.int32, (size, size), 1)
    identity = jnp.where(row == column, 1.0, 0.0).astype(jnp.float32)
    square = jnp.sum(gram * gram, axis=1, keepdims=True)
    scale = jnp.sqrt(jnp.sum(square, axis=0, keepdims=True) + 1e-06)
    current = gram / scale
    inverse = identity
    for repeat in range(NS_STEPS):
        if repeat == 0:
            middle = 1.5 * identity - 0.5 * current
        else:
            middle = 1.5 * identity - 0.5 * jnp.dot(inverse, current, precision=HIGHEST)
        if repeat < NS_STEPS - 1:
            current = jnp.dot(current, middle, precision=HIGHEST)
        inverse = middle if repeat == 0 else jnp.dot(middle, inverse, precision=HIGHEST)
    return inverse * jnp.sqrt(total / scale)


def split(x):
    high = x.astype(jnp.bfloat16)
    low = (x - high.astype(jnp.float32)).astype(jnp.bfloat16)
    return high, low


def kernel(wide, narrow, places, tile_hbm, start, out, stage, tile_hi, tile_lo, block,
           left, right, trans, direct, own, high, rowp, gath, pick, picked, tpart, dpart,
           placed, came, merged, last, grams, stage_sem, send_sem, recv_sem):
    me_w = lax.axis_index("wide")
    me_z = lax.axis_index("narrow")
    order = trans.shape[0]
    rows, width = own.shape[1], own.shape[2]
    half = rows // 2
    halves = narrow // 2
    wbits = bits_of(wide)
    hbits = bits_of(halves)
    two_orders = orders(wide)
    mate = flip(me_z, 1)
    wide_peers = [{"wide": flip(me_w, 1 << bit), "narrow": me_z} for bit in range(wbits)]
    near_peers = [
        {"wide": me_w, "narrow": flip(me_z, 1 << bit)} for bit in range(bits_of(narrow))
    ]

    barrier = pltpu.get_barrier_semaphore()
    for peer in wide_peers + near_peers:
        pl.semaphore_signal(
            barrier, inc=1, device_id=peer, device_id_type=pl.DeviceIdType.MESH
        )

    stage_rows = stage.shape[1]
    chunks = order // stage_rows

    def fetch(chunk):
        return pltpu.make_async_copy(
            tile_hbm.at[pl.ds(chunk * stage_rows, stage_rows)],
            stage.at[chunk % 2],
            stage_sem.at[chunk % 2],
        )

    fetch(0).start()
    if chunks > 1:
        fetch(1).start()
    pl.semaphore_wait(barrier, len(wide_peers) + len(near_peers))

    sent = []

    def send(source, target, peer):
        index = len(sent)
        copy = pltpu.make_async_remote_copy(
            src_ref=source,
            dst_ref=target,
            send_sem=send_sem.at[index],
            recv_sem=recv_sem.at[index],
            device_id=peer,
            device_id_type=pl.DeviceIdType.MESH,
        )
        copy.start()
        sent.append([copy, False])
        return len(sent) - 1

    def received(index):
        sent[index][0].wait_recv()

    def gone(index):
        if not sent[index][1]:
            sent[index][0].wait_send()
            sent[index][1] = True

    def natural(q):
        return pl.multiple_of(flip(me_z, q) * rows, rows)

    def load_tile():
        for chunk in range(chunks):
            fetch(chunk).wait()
            hi, lo = split(stage[chunk % 2])
            tile_hi[pl.ds(chunk * stage_rows, stage_rows), :] = hi
            tile_lo[pl.ds(chunk * stage_rows, stage_rows), :] = lo
            if chunk + 2 < chunks:
                fetch(chunk + 2).start()

    gram_peers = wide_peers + near_peers
    gram_state = {}

    def gram_begin(which, value):
        grams[which, 0] = value
        gram_state[which] = (0, send(grams.at[which, 0], grams.at[which, 1], gram_peers[0]))

    def gram_step(which):
        step, index = gram_state[which]
        received(index)
        total = grams[which, 2 * step] + grams[which, 2 * step + 1]
        step += 1
        if step == len(gram_peers):
            gram_state[which] = (step, None)
            return total
        grams[which, 2 * step] = total
        gram_state[which] = (
            step, send(grams.at[which, 2 * step], grams.at[which, 2 * step + 1], gram_peers[step])
        )
        return None

    total_rows = float(wide * order)
    step_of_columns = 256
    placed_sends = []
    merged_sends = []
    first_root = None

    for it in range(ITERS):
        high[it, 0] = start[...] if it == 0 else own[it]
        source = start if it == 0 else high.at[it, 0]
        far = []
        if halves > 1:
            far.append(send(source, high.at[it, 1], near_peers[1]))
        row_in = [None] * halves
        gathers = {}

        def begin(r):
            base = start if (it == 0 and r == 0) else high.at[it, r]
            row_in[r] = send(base, rowp.at[it, r], near_peers[0])
            for side in range(2):
                gath[it, side, r, 0] = high[it, r, pl.ds(side * half, half), :]
                gathers[r, side, 0] = send(
                    base.at[pl.ds(side * half, half)],
                    gath.at[it, side, r, 1],
                    wide_peers[two_orders[side][0]],
                )

        def advance(r, step):
            for side in range(2):
                received(gathers[r, side, step - 1])
                if step < wbits:
                    count = 1 << step
                    gathers[r, side, step] = send(
                        gath.at[it, side, r, pl.ds(0, count)],
                        gath.at[it, side, r, pl.ds(count, count)],
                        wide_peers[two_orders[side][step]],
                    )

        pick_in = [None] * halves

        def chosen(r, side, column):
            value = gath[it, side, r, 0]
            for p in range(1, wide):
                value = jnp.where(places[side, column] == p, gath[it, side, r, p], value)
            return value

        def choose(r):
            for side in range(2):
                pick[it, r, pl.ds(side * half, half), :] = chosen(r, side, mate)
            pick_in[r] = send(pick.at[it, r], picked.at[it, r], near_peers[0])

        def ready(r):
            if r == 0:
                return
            step = r.bit_length() - 1
            if r == 1 << step:
                received(far[step])
                if step + 1 < hbits:
                    count = 1 << (step + 1)
                    far.append(send(
                        high.at[it, pl.ds(0, count)],
                        high.at[it, pl.ds(count, count)],
                        near_peers[step + 2],
                    ))

        def transposed_terms():
            for r in range(halves):
                received(row_in[r])
                block[pl.ds(natural(2 * r), rows), :] = high[it, r]
                block[pl.ds(natural(2 * r + 1), rows), :] = rowp[it, r]
            turned = block[...].T
            hi, lo = split(turned)
            left[pl.ds(0, width), :] = hi
            left[pl.ds(width, width), :] = lo

            def body(chunk, carry):
                at = pl.multiple_of(chunk * step_of_columns, step_of_columns)
                both = jnp.dot(
                    left[...], tile_hi[:, pl.ds(at, step_of_columns)],
                    preferred_element_type=jnp.float32,
                )
                rest = jnp.dot(
                    left[pl.ds(0, width), :], tile_lo[:, pl.ds(at, step_of_columns)],
                    preferred_element_type=jnp.float32,
                )
                trans[pl.ds(at, step_of_columns), :] = (both[:width] + (both[width:] + rest)).T
                return carry

            lax.fori_loop(0, order // step_of_columns, body, 0)

        t_out = []
        d_out = []

        def direct_terms():
            for r in range(halves):
                received(pick_in[r])
                for side in range(2):
                    block[pl.ds(natural(2 * r) + side * half, half), :] = chosen(r, side, me_z)
                block[pl.ds(natural(2 * r + 1), rows), :] = picked[it, r]
            hi, lo = split(block[...])
            right[:, pl.ds(0, width)] = hi
            right[:, pl.ds(width, width)] = lo

            def body(chunk, carry):
                at = pl.multiple_of(chunk * step_of_columns, step_of_columns)
                both = jnp.dot(
                    tile_hi[pl.ds(at, step_of_columns), :], right[...],
                    preferred_element_type=jnp.float32,
                )
                rest = jnp.dot(
                    tile_lo[pl.ds(at, step_of_columns), :], right[:, pl.ds(0, width)],
                    preferred_element_type=jnp.float32,
                )
                direct[pl.ds(at, step_of_columns), :] = both[:, :width] + (both[:, width:] + rest)
                return carry

            lax.fori_loop(0, order // step_of_columns, body, 0)

        for time in range(halves + wbits + 1):
            for r in range(halves):
                step = time - r
                if step == 0:
                    ready(r)
                    begin(r)
                elif 0 < step <= wbits:
                    advance(r, step)
                    if step == wbits:
                        choose(r)
            if it == 0 and time == 0:
                load_tile()
            if it > 0 and 0 < time:
                if gram_state[0][1] is not None:
                    total = gram_step(0)
            if time == max(wbits, halves - 1):
                for index in t_out:
                    gone(index)
                transposed_terms()
                for r in range(halves - 1, -1, -1):
                    t_out.append(send(
                        trans.at[pl.ds(natural(2 * r + 1), rows)], tpart.at[it, r], near_peers[0]
                    ))
        direct_terms()
        for r in range(halves - 1, -1, -1):
            d_out.append(send(
                direct.at[pl.ds(natural(2 * r + 1), rows)], dpart.at[it, r], near_peers[0]
            ))
        if it > 0:
            while gram_state[0][1] is not None:
                total = gram_step(0)

        for index in placed_sends:
            gone(index)
        placed_sends = []
        sums = {}

        def put(r, side, first, count):
            mine = trans[pl.ds(natural(2 * r) + side * half, half), :]
            other = tpart[it, r, pl.ds(side * half, half), :]
            for p in range(first, first + count):
                placed[side, r, p] = jnp.where(places[side, me_z] == p, mine, 0.0) + jnp.where(
                    places[side, mate] == p, other, 0.0
                )

        def pass_on(r, side, step):
            count = 1 << step
            index = send(
                placed.at[side, r, pl.ds(count, count)],
                came.at[it, side, r, pl.ds(count, count)],
                wide_peers[two_orders[side][step]],
            )
            sums[r, side, step] = index
            placed_sends.append(index)

        for time in range(halves + wbits + 1):
            for turn in range(halves):
                r = halves - 1 - turn
                step = wbits - 1 - (time - turn)
                if step == wbits - 1:
                    received(t_out[turn])
                    for side in range(2):
                        put(r, side, wide // 2, wide // 2)
                        pass_on(r, side, step)
                    for side in range(2):
                        put(r, side, 0, wide // 2)
                elif -1 <= step < wbits - 1:
                    count = 1 << (step + 1)
                    for side in range(2):
                        received(sums[r, side, step + 1])
                        for p in range(count - 1, -1, -1):
                            placed[side, r, p] = placed[side, r, p] + came[it, side, r, count + p]
                        if step >= 0:
                            pass_on(r, side, step)
            if it > 0 and time == 0:
                first_root = inverse_root(total, total_rows)
                grams[0, 0 + 2 * len(gram_peers)] = first_root

        for turn in range(halves):
            r = halves - 1 - turn
            received(d_out[turn])
            for side in range(2):
                part = pl.ds(side * half, half)
                merged[it, r, part, :] = (
                    placed[side, r, 0]
                    + direct[pl.ds(natural(2 * r) + side * half, half), :]
                    + dpart[it, r, part, :]
                )
        for bit in range(hbits - 1, -1, -1):
            count = 1 << bit
            index = send(
                merged.at[it, pl.ds(count, count)],
                last.at[it, pl.ds(count, count)],
                near_peers[bit + 1],
            )
            received(index)
            for r in range(count):
                merged[it, r] = merged[it, r] + last[it, count + r]
        for index in t_out + d_out:
            gone(index)
        product = merged[it, 0]
        own[it + 1] = product
        turned = product.T
        gram_begin(it, jnp.dot(turned, product, precision=HIGHEST))

    root = grams[0, 2 * len(gram_peers)]
    total = None
    while total is None:
        total = gram_step(1)
    gram = jnp.dot(root.T, jnp.dot(total, root, precision=HIGHEST), precision=HIGHEST)
    root = jnp.dot(root, inverse_root(gram, total_rows), precision=HIGHEST)
    out[...] = jnp.dot(own[ITERS], root, precision=HIGHEST)
    for index in range(len(sent)):
        gone(index)


def on_device(hamiltonian_tiles, row_columns, start_vectors):
    wide, narrow = lax.axis_size("wide"), lax.axis_size("narrow")
    order = hamiltonian_tiles.shape[0]
    rows, width = start_vectors.shape
    assert rows * narrow == order
    halves = narrow // 2
    wbits, nbits = bits_of(wide), bits_of(narrow)
    relative = jnp.bitwise_xor(row_columns[0], lax.axis_index("wide").astype(jnp.int32))
    places = jnp.stack([position(relative, order_) for order_ in orders(wide)])
    copies = ITERS * (
        2 * (nbits - 1) + 4 * halves * wbits + 4 * halves
    ) + ITERS * (wbits + nbits)
    f32, bf16 = jnp.float32, jnp.bfloat16
    stage_rows = order // 6
    return pl.pallas_call(
        functools.partial(kernel, wide, narrow),
        out_shape=jax.ShapeDtypeStruct((rows, width), f32),
        in_specs=[
            pl.BlockSpec(memory_space=pltpu.SMEM),
            pl.BlockSpec(memory_space=pl.ANY),
            pl.BlockSpec(memory_space=pltpu.VMEM),
        ],
        out_specs=pl.BlockSpec(memory_space=pltpu.VMEM),
        scratch_shapes=[
            pltpu.VMEM((2, stage_rows, order), f32),
            pltpu.VMEM((order, order), bf16),
            pltpu.VMEM((order, order), bf16),
            pltpu.VMEM((order, width), f32),
            pltpu.VMEM((2 * width, order), bf16),
            pltpu.VMEM((order, 2 * width), bf16),
            pltpu.VMEM((order, width), f32),
            pltpu.VMEM((order, width), f32),
            pltpu.VMEM((ITERS + 1, rows, width), f32),
            pltpu.VMEM((ITERS, halves, rows, width), f32),
            pltpu.VMEM((ITERS, halves, rows, width), f32),
            pltpu.VMEM((ITERS, 2, halves, wide, rows // 2, width), f32),
            pltpu.VMEM((ITERS, halves, rows, width), f32),
            pltpu.VMEM((ITERS, halves, rows, width), f32),
            pltpu.VMEM((ITERS, halves, rows, width), f32),
            pltpu.VMEM((ITERS, halves, rows, width), f32),
            pltpu.VMEM((2, halves, wide, rows // 2, width), f32),
            pltpu.VMEM((ITERS, 2, halves, wide, rows // 2, width), f32),
            pltpu.VMEM((ITERS, halves, rows, width), f32),
            pltpu.VMEM((ITERS, halves, rows, width), f32),
            pltpu.VMEM((ITERS, 2 * (wbits + nbits) + 1, width, width), f32),
            pltpu.SemaphoreType.DMA((2,)),
            pltpu.SemaphoreType.DMA((copies,)),
            pltpu.SemaphoreType.DMA((copies,)),
        ],
        compiler_params=pltpu.CompilerParams(
            collective_id=0, has_side_effects=True, vmem_limit_bytes=67043328
        ),
    )(places, hamiltonian_tiles, start_vectors)


def solution(mesh):
    return jax.shard_map(
        on_device,
        mesh=mesh,
        in_specs=(P("wide", "narrow"), P("wide", None), P(("wide", "narrow"), None)),
        out_specs=P(("wide", "narrow"), None),
        check_vma=False,
    )
```

time: 500 us -> 167 us (0.33)
  waiting for transfers between devices: 309 us -> 0 us
  Pallas kernels: 0 us -> 162 us
  blocking collectives: 78.3 us -> 0 us
  matrix products: 65.2 us -> 0 us
  starting transfers between devices: 15.8 us -> 0 us
  between operations: 15.4 us -> 0.01 us
  local copies, waits for them, and re-layouts: 8.74 us -> 1.62 us
  other arithmetic: 6.83 us -> 1.23 us
    psum x2 -> x0, waiting for transfers between devices: 243 us -> none  [on_device(): gram = lax.psum(local_gram, ('wide', 'narrow'))]
    pallas_call x0 -> x1, Pallas kernels: none -> 162 us  [on_device(): pl.pallas_call(functools.partial(kernel, wide, narrow), out_shape=jax.Sha...]
    all_to_all x4 -> x0, waiting for transfers between devices: 65.7 us -> none  [the longest x2 32.9 us: on_device(): lax.all_to_all(transposed_spread, 'narrow', split_axis=0, concat_axis=0,...]
    dot_general x40 -> x0, matrix products: 65.2 us -> none  [the longest x2 26.6 us: on_device(): lax.dot_general(hamiltonian_tiles, row_block, (((0,), (0,)), ((), ())), p...]
    all_to_all x2 -> x0, blocking collectives: 43.1 us -> none  [on_device(): lax.all_to_all(direct_spread, 'narrow', split_axis=0, concat_axis=0, tile...]
    all_gather x2 -> x0, blocking collectives: 35.2 us -> none  [on_device(): gathered_rows = lax.all_gather(vectors, 'narrow', axis=0, tiled=True)]
    all_to_all x4 -> x0, starting transfers between devices: 15.1 us -> none  [the longest x2 8.16 us: on_device(): lax.all_to_all(transposed_spread, 'narrow', split_axis=0, concat_axis=0,...]
  transfers between devices with their start and end apart: 10 -> 0, of which waited for: 6 -> 0; matrix products, arithmetic and copies ran while one was open for 13% -> 0% of each run, Pallas kernels for 0% -> 0%
where the time goes in v1:
time: 167 us; the launch traced here: 164 us
  Pallas kernels  162 us (97%)
    pallas_call x1, Pallas kernels, on_device(): pl.pallas_call(functools.partial(kernel, wide, narrow), out_shape=jax.Sha...  162 us

profile of v1, /device:TPU:1, one launch (start us, length us, event | category | flops | bytes accessed | tf_op | source)
XLA Modules:
  0.0 164.5 jit_solution(4063232501684983852)
XLA Ops:
  0.0 0.7 add_add_fusion.1
  0.7 0.6 pad_add_fusion.places
  1.2 161.6 %shard_map.37 = f32[384,128]{1,0:T(8,128)} custom-call(s32[2,4]{1,0:T(2,128)} %pad_add_fusion.places, f32[1536,1536]{1,0:T(8,128)} %tile_hbm.1, f32[384,128]{1,0:T(8,128)} %start.1), custom_call_target="tpu_custom_call" | custom-call | tf_op jit(solution)/shard_map/pallas_call | solution.py:408
  162.9 1.6 copy.5

commit v2 on v1

v2 whole, which is shorter than its diff:
```python
import functools

import jax
import jax.numpy as jnp
from jax import lax
from jax.experimental import pallas as pl
from jax.experimental.pallas import tpu as pltpu
from jax.sharding import PartitionSpec as P

ITERS = 2
NS_STEPS = 5
HIGHEST = lax.Precision.HIGHEST


def flip(x, mask):
    bit = 1
    while bit <= mask:
        if mask & bit:
            x = x + bit * (1 - 2 * ((x // bit) % 2))
        bit *= 2
    return x


def bits_of(count):
    bits = count.bit_length() - 1
    assert count == 1 << bits
    return bits


def orders(wide):
    bits = list(range(1, bits_of(wide)))
    return bits + [0], bits[::-1] + [0]


def position(relative, order):
    return sum(((relative >> bit) & 1) << place for place, bit in enumerate(order))


def inverse_root(gram, total):
    size = gram.shape[0]
    row = lax.broadcasted_iota(jnp.int32, (size, size), 0)
    column = lax.broadcasted_iota(jnp.int32, (size, size), 1)
    identity = jnp.where(row == column, 1.0, 0.0).astype(jnp.float32)
    square = jnp.sum(gram * gram, axis=1, keepdims=True)
    scale = jnp.sqrt(jnp.sum(square, axis=0, keepdims=True) + 1e-06)
    current = gram / scale
    inverse = identity
    for repeat in range(NS_STEPS):
        if repeat == 0:
            middle = 1.5 * identity - 0.5 * current
        else:
            middle = 1.5 * identity - 0.5 * jnp.dot(inverse, current, precision=HIGHEST)
        if repeat < NS_STEPS - 1:
            current = jnp.dot(current, middle, precision=HIGHEST)
        inverse = middle if repeat == 0 else jnp.dot(middle, inverse, precision=HIGHEST)
    return inverse * jnp.sqrt(total / scale)


def split(x):
    high = x.astype(jnp.bfloat16)
    low = (x - high.astype(jnp.float32)).astype(jnp.bfloat16)
    return high, low


def kernel(wide, narrow, out_cuts, places, tile_hbm, start, out, stage, tile_hi, tile_lo, block, columns,
           left, right, trans, direct, own, high, rowp, gath, pick, picked, tpart, dpart,
           placed, came, merged, last, grams, stage_sem, send_sem, recv_sem):
    me_w = lax.axis_index("wide")
    me_z = lax.axis_index("narrow")
    order = trans.shape[0]
    rows, width = own.shape[1], own.shape[2]
    halves = narrow // 2
    wbits = bits_of(wide)
    hbits = bits_of(halves)
    two_orders = orders(wide)
    mate = flip(me_z, 1)
    wide_peers = [{"wide": flip(me_w, 1 << bit), "narrow": me_z} for bit in range(wbits)]
    near_peers = [
        {"wide": me_w, "narrow": flip(me_z, 1 << bit)} for bit in range(bits_of(narrow))
    ]

    barrier = pltpu.get_barrier_semaphore()
    for peer in wide_peers + near_peers:
        pl.semaphore_signal(
            barrier, inc=1, device_id=peer, device_id_type=pl.DeviceIdType.MESH
        )

    stage_rows = stage.shape[1]
    chunks = order // stage_rows

    def fetch(chunk):
        return pltpu.make_async_copy(
            tile_hbm.at[pl.ds(chunk * stage_rows, stage_rows)],
            stage.at[chunk % 2],
            stage_sem.at[chunk % 2],
        )

    fetch(0).start()
    if chunks > 1:
        fetch(1).start()
    pl.semaphore_wait(barrier, len(wide_peers) + len(near_peers))

    sent = []

    def send(source, target, peer):
        index = len(sent)
        copy = pltpu.make_async_remote_copy(
            src_ref=source,
            dst_ref=target,
            send_sem=send_sem.at[index],
            recv_sem=recv_sem.at[index],
            device_id=peer,
            device_id_type=pl.DeviceIdType.MESH,
        )
        copy.start()
        sent.append([copy, False])
        return len(sent) - 1

    def received(index):
        sent[index][0].wait_recv()

    def gone(index):
        if not sent[index][1]:
            sent[index][0].wait_send()
            sent[index][1] = True

    def natural(q):
        return pl.multiple_of(flip(me_z, q) * rows, rows)

    def load_chunk(chunk):
        fetch(chunk).wait()
        hi, lo = split(stage[chunk % 2])
        tile_hi[pl.ds(chunk * stage_rows, stage_rows), :] = hi
        tile_lo[pl.ds(chunk * stage_rows, stage_rows), :] = lo
        if chunk + 2 < chunks:
            fetch(chunk + 2).start()

    gram_peers = wide_peers + near_peers
    gram_state = {}

    def gram_begin(which, value):
        grams[which, 0] = value
        gram_state[which] = (0, send(grams.at[which, 0], grams.at[which, 1], gram_peers[0]))

    def gram_step(which):
        step, index = gram_state[which]
        received(index)
        total = grams[which, 2 * step] + grams[which, 2 * step + 1]
        step += 1
        if step == len(gram_peers):
            gram_state[which] = (step, None)
            return total
        grams[which, 2 * step] = total
        gram_state[which] = (
            step, send(grams.at[which, 2 * step], grams.at[which, 2 * step + 1], gram_peers[step])
        )
        return None

    total_rows = float(wide * order)
    step_of_columns = 256
    cuts = out_cuts
    piece = rows // cuts
    part = piece // 2
    units = [(r, c) for r in range(halves) for c in range(cuts)]
    back_units = [(r, c) for r in range(halves - 1, -1, -1) for c in range(cuts)]
    placed_sends = []
    total = None
    loaded = 0

    def whole_piece(c):
        return pl.ds(c * piece, piece)

    def side_rows(side):
        return pl.ds(side * part, part)

    for it in range(ITERS):
        far = {}
        row_in = {}
        pick_in = {}
        gathers = {}
        t_out = {}
        d_out = {}
        sums = {}
        ends = {}

        high[it, 0] = start[...] if it == 0 else own[it]
        source = start if it == 0 else high.at[it, 0]
        if halves > 1:
            for c in range(cuts):
                far[0, c] = send(
                    source.at[whole_piece(c)], high.at[it, 1, whole_piece(c)], near_peers[1]
                )

        def ready(r, c):
            if r == 0:
                return
            step = r.bit_length() - 1
            if r == 1 << step:
                received(far[step, c])
                if step + 1 < hbits:
                    count = 1 << (step + 1)
                    far[step + 1, c] = send(
                        high.at[it, pl.ds(0, count), whole_piece(c)],
                        high.at[it, pl.ds(count, count), whole_piece(c)],
                        near_peers[step + 2],
                    )

        def begin(r, c):
            base = source if r == 0 else high.at[it, r]
            for side in (2 * c, 2 * c + 1):
                gathers[r, side, 0] = send(
                    base.at[side_rows(side)],
                    gath.at[it, side, r, 1],
                    wide_peers[two_orders[side % 2][0]],
                )
            row_in[r, c] = send(
                base.at[whole_piece(c)], rowp.at[it, r, whole_piece(c)], near_peers[0]
            )
            for side in (2 * c, 2 * c + 1):
                gath[it, side, r, 0] = high[it, r, side_rows(side), :]

        def advance(r, c, step):
            for side in (2 * c, 2 * c + 1):
                received(gathers[r, side, step - 1])
                if step < wbits:
                    count = 1 << step
                    gathers[r, side, step] = send(
                        gath.at[it, side, r, pl.ds(0, count)],
                        gath.at[it, side, r, pl.ds(count, count)],
                        wide_peers[two_orders[side % 2][step]],
                    )

        def chosen(r, side, column):
            value = gath[it, side, r, 0]
            for p in range(1, wide):
                value = jnp.where(places[side % 2, column] == p, gath[it, side, r, p], value)
            return value

        def choose(r, c):
            for side in (2 * c, 2 * c + 1):
                pick[it, r, side_rows(side), :] = chosen(r, side, mate)
            pick_in[r, c] = send(
                pick.at[it, r, whole_piece(c)], picked.at[it, r, whole_piece(c)], near_peers[0]
            )
            for side in (2 * c, 2 * c + 1):
                columns[pl.ds(natural(2 * r) + side * part, part), :] = chosen(r, side, me_z)

        def transposed_terms():
            for r, c in units:
                received(row_in[r, c])
            for r in range(halves):
                block[pl.ds(natural(2 * r), rows), :] = high[it, r]
                block[pl.ds(natural(2 * r + 1), rows), :] = rowp[it, r]
            hi, lo = split(block[...].T)
            left[pl.ds(0, width), :] = hi
            left[pl.ds(width, width), :] = lo

            def body(chunk, carry):
                at = pl.multiple_of(chunk * step_of_columns, step_of_columns)
                both = jnp.dot(
                    left[...], tile_hi[:, pl.ds(at, step_of_columns)],
                    preferred_element_type=jnp.float32,
                )
                rest = jnp.dot(
                    left[pl.ds(0, width), :], tile_lo[:, pl.ds(at, step_of_columns)],
                    preferred_element_type=jnp.float32,
                )
                trans[pl.ds(at, step_of_columns), :] = (both[:width] + (both[width:] + rest)).T
                return carry

            lax.fori_loop(0, order // step_of_columns, body, 0)

        def direct_rows(q):
            at = natural(q)
            both = jnp.dot(
                tile_hi[pl.ds(at, rows), :], right[...], preferred_element_type=jnp.float32
            )
            rest = jnp.dot(
                tile_lo[pl.ds(at, rows), :], right[:, pl.ds(0, width)],
                preferred_element_type=jnp.float32,
            )
            direct[pl.ds(at, rows), :] = both[:, :width] + (both[:, width:] + rest)

        def send_rows(results, landing, group, r):
            for c in range(cuts):
                group[r, c] = send(
                    results.at[pl.ds(natural(2 * r + 1) + c * piece, piece)],
                    landing.at[it, r, whole_piece(c)],
                    near_peers[0],
                )

        def step_gram():
            return gram_step(it - 1) if it > 0 and gram_state[it - 1][1] is not None else None

        for time in range(len(units) + wbits):
            for place in range(len(units)):
                r, c = units[place]
                step = time - place
                if step == 0:
                    ready(r, c)
                    begin(r, c)
                elif 0 < step <= wbits:
                    advance(r, c, step)
                    if step == wbits:
                        choose(r, c)
            if it == 0 and loaded < chunks:
                load_chunk(loaded)
                loaded += 1
            if time % 2 == 1:
                found = step_gram()
                total = found if found is not None else total
        while loaded < chunks:
            load_chunk(loaded)
            loaded += 1

        transposed_terms()
        send_rows(trans, tpart, t_out, halves - 1)
        for r, c in units:
            received(pick_in[r, c])
        for r in range(halves):
            columns[pl.ds(natural(2 * r + 1), rows), :] = picked[it, r]
        hi, lo = split(columns[...])
        right[:, pl.ds(0, width)] = hi
        right[:, pl.ds(width, width)] = lo
        for r in range(halves - 1, -1, -1):
            direct_rows(2 * r + 1)
            send_rows(direct, dpart, d_out, r)
            if r > 0:
                send_rows(trans, tpart, t_out, r - 1)
        for r in range(halves - 1, -1, -1):
            direct_rows(2 * r)

        for index in placed_sends:
            gone(index)
        placed_sends = []

        def put(r, side, first, count):
            mine = trans[pl.ds(natural(2 * r) + side * part, part), :]
            other = tpart[it, r, side_rows(side), :]
            for p in range(first, first + count):
                placed[side, r, p] = jnp.where(
                    places[side % 2, me_z] == p, mine, 0.0
                ) + jnp.where(places[side % 2, mate] == p, other, 0.0)

        def pass_on(r, side, step):
            count = 1 << step
            index = send(
                placed.at[side, r, pl.ds(count, count)],
                came.at[it, side, r, pl.ds(count, count)],
                wide_peers[two_orders[side % 2][step]],
            )
            sums[r, side, step] = index
            placed_sends.append(index)

        def merge(r, c):
            received(d_out[r, c])
            for side in (2 * c, 2 * c + 1):
                at = side_rows(side)
                merged[it, r, at, :] = (
                    placed[side, r, 0]
                    + direct[pl.ds(natural(2 * r) + side * part, part), :]
                    + dpart[it, r, at, :]
                )
            if r >= max(1, halves // 2):
                ends[r, c] = send(
                    merged.at[it, r, whole_piece(c)],
                    last.at[it, r, whole_piece(c)],
                    near_peers[hbits],
                )

        for time in range(len(back_units) + wbits):
            for place in range(len(back_units)):
                r, c = back_units[place]
                step = wbits - 1 - (time - place)
                sides = (2 * c, 2 * c + 1)
                if step == wbits - 1:
                    received(t_out[r, c])
                    for side in sides:
                        put(r, side, wide // 2, wide // 2)
                        pass_on(r, side, step)
                    for side in sides:
                        put(r, side, 0, wide // 2)
                elif -1 <= step < wbits - 1:
                    count = 1 << (step + 1)
                    for side in sides:
                        received(sums[r, side, step + 1])
                        for p in range(count - 1, -1, -1):
                            placed[side, r, p] = placed[side, r, p] + came[it, side, r, count + p]
                        if step >= 0:
                            pass_on(r, side, step)
                    if step < 0:
                        merge(r, c)
            if time % 2 == 1:
                found = step_gram()
                total = found if found is not None else total
        if it > 0:
            while gram_state[it - 1][1] is not None:
                total = gram_step(it - 1)
            grams[0, 2 * len(gram_peers)] = inverse_root(total, total_rows)

        for r, c in ends:
            received(ends[r, c])
            merged[it, r - halves // 2, whole_piece(c), :] = (
                merged[it, r - halves // 2, whole_piece(c), :] + last[it, r, whole_piece(c), :]
            )
        for bit in range(hbits - 2, -1, -1):
            count = 1 << bit
            received(send(
                merged.at[it, pl.ds(count, count)],
                last.at[it, pl.ds(count, count)],
                near_peers[bit + 1],
            ))
            for r in range(count):
                merged[it, r] = merged[it, r] + last[it, count + r]
        for index in list(t_out.values()) + list(d_out.values()):
            gone(index)
        product = merged[it, 0]
        own[it + 1] = product
        gram_now = jnp.dot(product.T, product, precision=HIGHEST)
        gram_begin(it, gram_now)

    root = grams[0, 2 * len(gram_peers)]
    total = None
    while total is None:
        total = gram_step(1)
    gram = jnp.dot(root.T, jnp.dot(total, root, precision=HIGHEST), precision=HIGHEST)
    root = jnp.dot(root, inverse_root(gram, total_rows), precision=HIGHEST)
    out[...] = jnp.dot(own[ITERS], root, precision=HIGHEST)
    for index in range(len(sent)):
        gone(index)


def on_device(hamiltonian_tiles, row_columns, start_vectors):
    wide, narrow = lax.axis_size("wide"), lax.axis_size("narrow")
    order = hamiltonian_tiles.shape[0]
    rows, width = start_vectors.shape
    assert rows * narrow == order
    halves = narrow // 2
    wbits, nbits = bits_of(wide), bits_of(narrow)
    relative = jnp.bitwise_xor(row_columns[0], lax.axis_index("wide").astype(jnp.int32))
    places = jnp.stack([position(relative, order_) for order_ in orders(wide)])
    cuts = 2 if halves <= 2 else 1
    copies = ITERS * (
        2 * cuts * nbits + (4 * wbits + 5) * halves * cuts
    ) + ITERS * (wbits + nbits)
    f32, bf16 = jnp.float32, jnp.bfloat16
    stage_rows = order // 6
    return pl.pallas_call(
        functools.partial(kernel, wide, narrow, cuts),
        out_shape=jax.ShapeDtypeStruct((rows, width), f32),
        in_specs=[
            pl.BlockSpec(memory_space=pltpu.SMEM),
            pl.BlockSpec(memory_space=pl.ANY),
            pl.BlockSpec(memory_space=pltpu.VMEM),
        ],
        out_specs=pl.BlockSpec(memory_space=pltpu.VMEM),
        scratch_shapes=[
            pltpu.VMEM((2, stage_rows, order), f32),
            pltpu.VMEM((order, order), bf16),
            pltpu.VMEM((order, order), bf16),
            pltpu.VMEM((order, width), f32),
            pltpu.VMEM((order, width), f32),
            pltpu.VMEM((2 * width, order), bf16),
            pltpu.VMEM((order, 2 * width), bf16),
            pltpu.VMEM((order, width), f32),
            pltpu.VMEM((order, width), f32),
            pltpu.VMEM((ITERS + 1, rows, width), f32),
            pltpu.VMEM((ITERS, halves, rows, width), f32),
            pltpu.VMEM((ITERS, halves, rows, width), f32),
            pltpu.VMEM((ITERS, 2 * cuts, halves, wide, rows // (2 * cuts), width), f32),
            pltpu.VMEM((ITERS, halves, rows, width), f32),
            pltpu.VMEM((ITERS, halves, rows, width), f32),
            pltpu.VMEM((ITERS, halves, rows, width), f32),
            pltpu.VMEM((ITERS, halves, rows, width), f32),
            pltpu.VMEM((2 * cuts, halves, wide, rows // (2 * cuts), width), f32),
            pltpu.VMEM((ITERS, 2 * cuts, halves, wide, rows // (2 * cuts), width), f32),
            pltpu.VMEM((ITERS, halves, rows, width), f32),
            pltpu.VMEM((ITERS, halves, rows, width), f32),
            pltpu.VMEM((ITERS, 2 * (wbits + nbits) + 1, width, width), f32),
            pltpu.SemaphoreType.DMA((2,)),
            pltpu.SemaphoreType.DMA((copies,)),
            pltpu.SemaphoreType.DMA((copies,)),
        ],
        compiler_params=pltpu.CompilerParams(
            collective_id=0, has_side_effects=True, vmem_limit_bytes=67043328
        ),
    )(places, hamiltonian_tiles, start_vectors)


def solution(mesh):
    return jax.shard_map(
        on_device,
        mesh=mesh,
        in_specs=(P("wide", "narrow"), P("wide", None), P(("wide", "narrow"), None)),
        out_specs=P(("wide", "narrow"), None),
        check_vma=False,
    )
```

time: 167 us -> 141 us (0.84)
  Pallas kernels: 162 us -> 136 us
    pallas_call x1, Pallas kernels: 162 us -> 136 us  [on_device(): pl.pallas_call(functools.partial(kernel, wide, narrow, cuts), out_shape=j...]
where the time goes in v2:
time: 141 us; the launch traced here: 139 us
  Pallas kernels  136 us (96%)
  local copies, waits for them, and re-layouts  1.62 us (1%)
    pallas_call x1, Pallas kernels, on_device(): pl.pallas_call(functools.partial(kernel, wide, narrow, cuts), out_shape=j...  136 us

profile of v2, /device:TPU:1, one launch (start us, length us, event | category | flops | bytes accessed | tf_op | source)
XLA Modules:
  0.0 138.6 jit_solution(8184143604849942457)
XLA Ops:
  0.0 0.7 add_add_fusion.1
  0.7 0.6 pad_add_fusion.places
  1.2 135.7 %shard_map.37 = f32[384,128]{1,0:T(8,128)} custom-call(s32[2,4]{1,0:T(2,128)} %pad_add_fusion.places, f32[1536,1536]{1,0:T(8,128)} %tile_hbm.1, f32[384,128]{1,0:T(8,128)} %start.1), custom_call_target="tpu_custom_call" | custom-call | tf_op jit(solution)/shard_map/pallas_call | solution.py:448
  137.0 1.6 %copy.5 = f32[384,128]{1,0:T(8,128)} copy(f32[384,128]{1,0:T(8,128)} %shard_map.37) | data formatting | bytes 393216
